TPU v7x, 512 devices: a whole 4x4x16 slice. The times are simulated.
512 devices in a mesh: comp: 16 (over z_lo, core), feat: 32 (over x, y, z_hi).
Axes of the slice: x: 4, y: 4, z: 16 (z_hi: 2, z_lo: 8; z = z_hi * 8 + z_lo), core: 2. Of those that a mesh axis runs over, the one named last changes fastest.
Arguments:
- samples: float32 [1, 192, 28672], P(None, None, 'feat'), may hold values from -20 to 20, as said below
- start_vectors: float32 [1024, 28672], P('comp', 'feat'), may hold values from -8 to 8
Outputs:
- vectors: float32 [1024, 28672], P('comp', 'feat')
Inputs may be any that keep to these rules, and one draw needn't show every extreme that they name: `samples`: activation rows with feature scales that differ over a factor of ten.
All inputs are finite; a program needn't handle non-finite values.
Results may differ from a plain program's by a relative error of at most 0.0001.
Values sent between devices are 32-bit elements; how exact they have to be, the bound alone decides.
A program may use at most 64 MiB of HBM per device.

v0:
```python
import math

import jax
import jax.numpy as jnp
from jax import lax
from jax.sharding import PartitionSpec as P

step_rate = 0.1
epsilon = 1e-06
highest = lax.Precision.HIGHEST


def project(sample, vectors, root_width):
    return jnp.einsum("rd,kd->rk", sample, vectors, precision=highest) / root_width


def normalize(updated, features):
    summed = lax.psum(jnp.sum(updated * updated, axis=1), "feat")
    return updated * lax.rsqrt(summed / features + epsilon)[:, None]


def couplings(every_images, own_images, earlier):
    intersection = (
        jnp.einsum("rj,ri->ji", every_images, own_images, precision=highest) / own_images.shape[0]
    )
    return jnp.where(earlier, intersection, jnp.float32(0.0))


def shards(samples, start_vectors):
    per_group = start_vectors.shape[0]
    features = samples.shape[2] * lax.axis_size("feat")
    total_rows = per_group * lax.axis_size("comp")
    root_width = math.sqrt(features)
    group_index = lax.axis_index("comp")
    own_columns = group_index * per_group + jnp.arange(per_group, dtype=jnp.int32)
    earlier = jnp.arange(total_rows, dtype=jnp.int32)[:, None] < own_columns[None, :]
    current = normalize(start_vectors, features)
    sample = samples[0]
    gathered = lax.all_gather(current, "comp", axis=0, tiled=True)
    every_images = lax.psum(project(sample, gathered, root_width), "feat")
    own_images = lax.dynamic_slice_in_dim(every_images, group_index * per_group, per_group, 1)
    vector = lax.dynamic_slice_in_dim(gathered, group_index * per_group, per_group, 0)
    coupling = couplings(every_images, own_images, earlier)
    penalty = jnp.einsum("ji,jd->id", coupling, gathered, precision=highest)
    gradient = (
        root_width
        * jnp.einsum("rk,rd->kd", own_images, sample, precision=highest)
        / sample.shape[0]
        - penalty
    )
    current = vector + step_rate * gradient
    current = normalize(current, features)
    return current


def solution(mesh):
    in_specs = (P(None, None, "feat"), P("comp", "feat"))
    out_specs = P("comp", "feat")
    return jax.shard_map(shards, mesh=mesh, in_specs=in_specs, out_specs=out_specs, check_vma=False)
```

profile of v0, /device:TPU:32, one launch (start us, length us, event | category | flops | bytes accessed | tf_op | source)
XLA Modules:
  0.0 1033.8 jit_solution(12767098209797000956)
XLA Ops:
  6.5 0.0 copy-start
  6.5 0.0 all-gather.2.cloned.1.call-start
  6.5 1.1 multiply_reduce_fusion.1
  7.7 164.5 %psum.21 = f32[64]{0:T(128)S(1)} all-reduce(f32[64]{0:T(128)S(1)} %multiply_reduce_fusion.1), channel_id=1, replica_groups=mesh['comp'=16,'feat'=32] {'feat'}, use_global_device_ids=true, to_apply=%region_1.0 | all-reduce | flops 64 | bytes 512 | tf_op jit(solution)/shard_map/psum | solution.py:18
  172.1 1.7 broadcast_multiply_fusion.1
  173.8 0.0 all-gather.2.cloned.1.call-update
  173.9 0.0 all-reduce.2.cloned.1.call-start
  173.9 86.6 %all-gather.2.cloned.1.call-done = f32[1024,896]{1,0:T(8,128)} async-done(((f32[64,896]{1,0:T(8,128)}), f32[1024,896]{1,0:T(8,128)}) %all-gather.2.cloned.1.call-update) | async-done | bytes 3670032 | tf_op jit(solution)/shard_map/all_gather | solution.py:39
  260.5 0.0 copy-done
  260.5 6.9 fusion
  267.4 0.0 all-reduce.2.cloned.1.call-update
  267.5 591.4 %all-reduce.2.cloned.1.call-done = f32[192,1024]{1,0:T(8,128)} async-done(((f32[192,1024]{1,0:T(8,128)}), f32[192,1024]{1,0:T(8,128)}) %all-reduce.2.cloned.1.call-update) | async-done | bytes 786448 | tf_op jit(solution)/shard_map/psum | solution.py:40
  858.8 3.0 fusion.1
  861.8 4.3 fusion.11
  866.1 1.8 multiply_reduce_fusion
  867.9 158.3 %psum.23 = f32[64]{0:T(128)S(1)} all-reduce(f32[64]{0:T(128)S(1)} %get-tuple-element.5), channel_id=1, replica_groups=mesh['comp'=16,'feat'=32] {'feat'}, use_global_device_ids=true, to_apply=%region_4.5 | all-reduce | flops 64 | bytes 512 | tf_op jit(solution)/shard_map/psum | solution.py:18
  1026.2 0.8 broadcast_multiply_fusion
  (3 shorter events, 0.0 us)
Async XLA Ops:
  6.5 254.0 %copy-start = (f32[1,192,896]{2,1,0:T(8,128)S(1)}, f32[1,192,896]{2,1,0:T(8,128)}, u32[]{:S(2)}) copy-start(f32[1,192,896]{2,1,0:T(8,128)} %param.2) | copy-start | bytes 2064388
  6.5 254.0 %all-gather.2.cloned.1.call-start = ((), (), s32[]{:S(2)}) async-start(), calls=%async_computation | async-start | bytes 3899392 | tf_op jit(solution)/shard_map/all_gather | solution.py:39
  173.9 684.9 %all-reduce.2.cloned.1.call-start = ((), (), s32[]{:S(2)}) async-start(), calls=%async_computation.1 | async-start | bytes 1572864 | tf_op jit(solution)/shard_map/psum | solution.py:40
Sparse Core Ops, SparseCore 0:
  174.0 86.4 all-gather.1
  267.6 591.2 all-reduce.1
where the time goes:
time: 1030 us
  waiting for transfers between devices  678 us (66%)
  blocking collectives  323 us (31%)
  matrix products  16 us (2%)
  between operations  13.4 us (1%)
    psum x1, waiting for transfers between devices, shards(): every_images = lax.psum(project(sample, gathered, root_width), 'feat')  591 us
    psum x2, blocking collectives, normalize(): summed = lax.psum(jnp.sum(updated * updated, axis=1), 'feat')  323 us
    all_gather x1, waiting for transfers between devices, shards(): gathered = lax.all_gather(current, 'comp', axis=0, tiled=True)  86.6 us
  transfers between devices with their start and end apart: 2, of which 2 were waited for; matrix products, arithmetic and copies ran while one was open for 0% of the time, Pallas kernels for 0%

commit v1 on v0

v1 whole, which is shorter than its diff:
```python
import functools
import math

import jax
import jax.numpy as jnp
from jax import lax
from jax.experimental import pallas as pl
from jax.experimental.pallas import tpu as pltpu
from jax.sharding import PartitionSpec as P

MESH = pl.DeviceIdType.MESH
step_rate = 0.1
epsilon = 1e-06
highest = lax.Precision.HIGHEST

GEOMETRY = dict(planes=16, highs=2, lows=8)
SUB = 24


def dot(a, b, ca, cb):
    return lax.dot_general(
        a, b, (((ca,), (cb,)), ((), ())), precision=highest, preferred_element_type=jnp.float32
    )


def landed(ref, sem):
    pltpu.make_async_copy(ref, ref, sem).wait()


def kernel(
    planes, highs, lows, sub, features,
    s_hbm, u_hbm, out_ref,
    s_v, u_pad, u_chip, p_v, rs_v, zs_v, zr_v, tot_v, x_v, v_v, xt_v, ct_v, own_v, in_v, o_v, new_v, fin_v,
    ld_sem, ux_send, ux_recv, rs_send, rs_recv, z_send, z_recv, ag_send, ag_recv,
    ch_send, ch_recv, rl_send, rl_recv, fin_send, fin_recv,
):
    rows, width = s_v.shape
    half = rows // 2
    tiles = half // 8 + 1
    group = 64
    blocks = width // 128
    subs = half // sub
    feats = planes * highs
    root = math.sqrt(features)

    comp = lax.axis_index("comp")
    feat = lax.axis_index("feat")
    core = lax.rem(comp, 2)
    low = lax.div(comp, 2)
    high = lax.rem(feat, highs)
    plane = lax.div(feat, highs)
    partner = (low * 2 + 1 - core, feat)
    first = low == 0
    last = low == lows - 1
    mine = plane < tiles
    my_rows = pl.multiple_of(core * half, 8)

    load_s = pltpu.make_async_copy(s_hbm.at[0], s_v, ld_sem.at[0])
    load_u = pltpu.make_async_copy(u_hbm, u_pad.at[pl.ds(group, group)], ld_sem.at[1])
    own_group = pl.ds(pl.multiple_of(core * group, 8), group)
    load_c = pltpu.make_async_copy(u_hbm, u_chip.at[own_group], ld_sem.at[2])
    load_u.start()
    load_s.start()
    load_c.start()

    barrier = pltpu.get_barrier_semaphore()

    def plane_peer(d):
        q = lax.rem(plane * 2 + core + d, 2 * planes)
        p = lax.div(q, 2)
        return low * 2 + lax.rem(q, 2), p * highs + high

    def greet(d, carry):
        pl.semaphore_signal(barrier, inc=1, device_id=plane_peer(d), device_id_type=MESH)
        return carry

    across = (comp, plane * highs + 1 - high)
    right = (comp + 2, feat)
    left = (comp - 2, feat)
    pl.semaphore_signal(barrier, inc=1, device_id=across, device_id_type=MESH)
    lax.fori_loop(1, 2 * planes, greet, 0)

    @pl.when(jnp.logical_not(first))
    def _():
        pl.semaphore_signal(barrier, inc=1, device_id=left, device_id_type=MESH)

    @pl.when(jnp.logical_not(last))
    def _():
        pl.semaphore_signal(barrier, inc=1, device_id=right, device_id_type=MESH)

    u_pad[0:group, :] = jnp.zeros((group, width), jnp.float32)
    u_pad[2 * group : 3 * group, :] = jnp.zeros((group, width), jnp.float32)
    load_u.wait()
    u_own = u_pad[group : 2 * group, :]
    squares = jnp.zeros((group, 128), jnp.float32)
    for b in range(blocks):
        piece = u_own[:, b * 128 : (b + 1) * 128]
        squares = squares + piece * piece
    squares = jnp.concatenate([squares, squares], axis=0)
    p_v[tiles - 1] = dot(jnp.ones((8, 128), jnp.float32), squares, 1, 1)
    load_s.wait()
    projected = dot(s_v[0:half, :], u_pad[group : 3 * group, :], 1, 1) + dot(
        s_v[half:rows, :], u_pad[0 : 2 * group, :], 1, 1
    )
    for t in range(tiles - 1):
        p_v[t] = projected[8 * t : 8 * t + 8, :]

    pl.semaphore_wait(
        barrier,
        2 * planes
        + jnp.where(first, 0, 1).astype(jnp.int32)
        + jnp.where(last, 0, 1).astype(jnp.int32),
    )

    def scatter(t, wait):
        copy = pltpu.make_async_remote_copy(
            src_ref=p_v.at[t],
            dst_ref=rs_v.at[plane],
            send_sem=rs_send.at[t],
            recv_sem=rs_recv.at[plane],
            device_id=(comp, t * highs + high),
            device_id_type=MESH,
        )

        @pl.when(t != plane)
        def _():
            if wait:
                copy.wait_send()
            else:
                copy.start()

    def scatter_start(t, carry):
        scatter(t, False)
        return carry

    lax.fori_loop(0, tiles, scatter_start, 0)

    load_c.wait()
    to_partner = pltpu.make_async_remote_copy(
        src_ref=u_chip.at[own_group],
        dst_ref=u_chip.at[own_group],
        send_sem=ux_send,
        recv_sem=ux_recv,
        device_id=partner,
        device_id_type=MESH,
    )
    to_partner.start()

    exchange = pltpu.make_async_remote_copy(
        src_ref=zs_v, dst_ref=zr_v, send_sem=z_send, recv_sem=z_recv, device_id=across, device_id_type=MESH
    )

    def spread(d):
        return pltpu.make_async_remote_copy(
            src_ref=tot_v,
            dst_ref=x_v.at[core, plane],
            send_sem=ag_send.at[d],
            recv_sem=ag_recv.at[core, plane],
            device_id=plane_peer(d),
            device_id_type=MESH,
        )

    @pl.when(mine)
    def _():
        rs_v[plane] = p_v[plane]

        def arrive(p, carry):
            @pl.when(p != plane)
            def _():
                landed(rs_v.at[p], rs_recv.at[p])

            return carry

        lax.fori_loop(0, planes, arrive, 0)
        total = rs_v[0]
        for p in range(1, planes):
            total = total + rs_v[p]
        zs_v[...] = total
        exchange.start()
        exchange.wait_recv()
        total = zs_v[...] + zr_v[...]
        tot_v[...] = total

        def spread_start(d, carry):
            spread(d).start()
            return carry

        lax.fori_loop(1, 2 * planes, spread_start, 0)
        x_v[core, plane] = total

    landed(u_chip.at[pl.ds(pl.multiple_of((1 - core) * group, 8), group)], ux_recv)
    to_partner.wait_send()

    def gathered(i, carry):
        g = lax.div(i, tiles)
        t = lax.rem(i, tiles)

        @pl.when(jnp.logical_or(g != core, t != plane))
        def _():
            landed(x_v.at[g, t], ag_recv.at[g, t])

        return carry

    lax.fori_loop(0, 2 * tiles, gathered, 0)

    lane = lax.broadcasted_iota(jnp.int32, (8, 128), 1)
    scale0 = lax.rsqrt(x_v[0, tiles - 1] / features + epsilon)
    scale1 = lax.rsqrt(x_v[1, tiles - 1] / features + epsilon)
    scale_row = jnp.where(lane < group, scale0, scale1)
    for t in range(tiles - 1):
        x0 = x_v[0, t] * scale0 / root
        x1 = x_v[1, t] * scale1 / root
        a = jnp.where(lane < group, x0, pltpu.roll(x1, 64, 1))
        b = jnp.where(lane < group, pltpu.roll(x0, 64, 1), x1)
        rs_rows = pl.ds(8 * t, 8)
        xc_rows = pl.ds(half + 8 * t, 8)
        xt_v[rs_rows, :] = a
        xt_v[xc_rows, :] = b
    eye = lax.broadcasted_iota(jnp.int32, (128, 128), 0) == lax.broadcasted_iota(jnp.int32, (128, 128), 1)
    scale_col = jnp.sum(
        jnp.where(eye, jnp.broadcast_to(scale_row[0:1, :], (128, 128)), 0.0), axis=1, keepdims=True
    )
    v_v[...] = u_chip[...] * scale_col
    x_half = xt_v[pl.ds(my_rows, half), :]
    for b in range(blocks):
        own_v[b] = dot(x_half, v_v[:, b * 128 : (b + 1) * 128], 1, 0)

    def base():
        x_chip = xt_v[...]
        pairs = dot(x_chip, x_chip, 0, 0) / rows
        i = lax.broadcasted_iota(jnp.int32, (128, 128), 0)
        j = lax.broadcasted_iota(jnp.int32, (128, 128), 1)
        ct_v[...] = jnp.where(j < i, pairs, 0.0)
        pull = dot(x_chip, s_v[...], 0, 0) * (root / rows) - dot(ct_v[...], v_v[...], 1, 0)
        u_chip[...] = v_v[...] + step_rate * pull
        new_v[...] = u_chip[own_group, :]

    early = low >= lows // 2 - 1

    @pl.when(early)
    def _():
        base()

    def hop(b, s):
        i = b * subs + s
        here = pl.ds(pl.multiple_of(my_rows + s * sub, 8), sub)
        there = pl.ds(pl.multiple_of(s * sub, 8), sub)
        forward = pltpu.make_async_remote_copy(
            src_ref=o_v.at[b, there],
            dst_ref=in_v.at[b, here],
            send_sem=ch_send.at[i],
            recv_sem=ch_recv.at[i],
            device_id=right,
            device_id_type=MESH,
        )
        relay = pltpu.make_async_remote_copy(
            src_ref=in_v.at[b, here],
            dst_ref=in_v.at[b, here],
            send_sem=rl_send.at[i],
            recv_sem=rl_recv.at[i],
            device_id=partner,
            device_id_type=MESH,
        )
        return here, there, forward, relay

    def finish(b):
        def arrived(s, carry):
            other = pl.ds(pl.multiple_of((1 - core) * half + s * sub, 8), sub)
            landed(in_v.at[b, other], rl_recv.at[b * subs + s])
            return carry

        lax.fori_loop(0, subs, arrived, 0)
        pull = dot(xt_v[...], in_v[b], 0, 0) * (step_rate / rows)
        ct_v[...] = pull
        columns = pl.ds(pl.multiple_of(b * 128, 128), 128)
        new_v[:, columns] = new_v[:, columns] - ct_v[own_group, :]

    def chain(b, carry):
        def one(s, carry):
            here, there, forward, relay = hop(b, s)

            @pl.when(first)
            def _():
                o_v[b, there] = own_v[b, there]
                forward.start()

            @pl.when(jnp.logical_not(first))
            def _():
                landed(in_v.at[b, here], ch_recv.at[b * subs + s])

                @pl.when(jnp.logical_not(last))
                def _():
                    o_v[b, there] = in_v[b, here] + own_v[b, there]
                    forward.start()

                relay.start()

            return carry

        lax.fori_loop(0, subs, one, 0)

        @pl.when(jnp.logical_and(last, b > 0))
        def _():
            finish(b - 1)

        return carry

    lax.fori_loop(0, blocks, chain, 0)

    @pl.when(last)
    def _():
        finish(blocks - 1)

    @pl.when(jnp.logical_not(early))
    def _():
        base()

    @pl.when(jnp.logical_not(jnp.logical_or(first, last)))
    def _():
        def finish_all(b, carry):
            finish(b)
            return carry

        lax.fori_loop(0, blocks, finish_all, 0)

    squares = jnp.zeros((group, 128), jnp.float32)
    for b in range(blocks):
        piece = new_v[:, b * 128 : (b + 1) * 128]
        squares = squares + piece * piece
    column = jnp.sum(squares, axis=1, keepdims=True)
    eye_half = lax.broadcasted_iota(jnp.int32, (group, 128), 0) == lax.broadcasted_iota(
        jnp.int32, (group, 128), 1
    )
    fin_v[feat] = jnp.sum(jnp.where(eye_half, column, 0.0), axis=0, keepdims=True)

    def tell(d):
        q = lax.rem(feat + d, feats)
        return pltpu.make_async_remote_copy(
            src_ref=fin_v.at[feat],
            dst_ref=fin_v.at[feat],
            send_sem=fin_send.at[d],
            recv_sem=fin_recv.at[feat],
            device_id=(comp, q),
            device_id_type=MESH,
        )

    def tell_start(d, carry):
        tell(d).start()
        return carry

    lax.fori_loop(1, feats, tell_start, 0)

    def told(d, carry):
        q = lax.rem(feat + d, feats)
        landed(fin_v.at[q], fin_recv.at[q])
        return carry

    lax.fori_loop(1, feats, told, 0)
    total = fin_v[0]
    for q in range(1, feats):
        total = total + fin_v[q]
    scale = lax.rsqrt(
        jnp.sum(jnp.where(eye_half, jnp.broadcast_to(total, (group, 128)), 0.0), axis=1, keepdims=True)
        / features
        + epsilon
    )
    out_ref[...] = new_v[...] * scale

    def scatter_end(t, carry):
        scatter(t, True)
        return carry

    lax.fori_loop(0, tiles, scatter_end, 0)

    @pl.when(mine)
    def _():
        exchange.wait_send()

        def spread_end(d, carry):
            spread(d).wait_send()
            return carry

        lax.fori_loop(1, 2 * planes, spread_end, 0)

    def chain_end(i, carry):
        here, there, forward, relay = hop(lax.div(i, subs), lax.rem(i, subs))

        @pl.when(jnp.logical_not(last))
        def _():
            forward.wait_send()

        @pl.when(jnp.logical_not(first))
        def _():
            relay.wait_send()

        return carry

    lax.fori_loop(0, blocks * subs, chain_end, 0)

    def tell_end(d, carry):
        tell(d).wait_send()
        return carry

    lax.fori_loop(1, feats, tell_end, 0)


def step(planes, highs, lows, sub, samples, start_vectors):
    _, rows, width = samples.shape
    group = start_vectors.shape[0]
    feats = planes * highs
    half = rows // 2
    tiles = half // 8 + 1
    blocks = width // 128
    chunks = blocks * (half // sub)
    dma = pltpu.SemaphoreType.DMA
    f32 = jnp.float32
    return pl.pallas_call(
        functools.partial(kernel, planes, highs, lows, sub, width * feats),
        out_shape=jax.ShapeDtypeStruct((group, width), f32),
        in_specs=[pl.BlockSpec(memory_space=pl.ANY)] * 2,
        out_specs=pl.BlockSpec(memory_space=pltpu.VMEM),
        scratch_shapes=[
            pltpu.VMEM((rows, width), f32),
            pltpu.VMEM((3 * group, width), f32),
            pltpu.VMEM((2 * group, width), f32),
            pltpu.VMEM((tiles, 8, 128), f32),
            pltpu.VMEM((planes, 8, 128), f32),
            pltpu.VMEM((8, 128), f32),
            pltpu.VMEM((8, 128), f32),
            pltpu.VMEM((8, 128), f32),
            pltpu.VMEM((2, tiles, 8, 128), f32),
            pltpu.VMEM((2 * group, width), f32),
            pltpu.VMEM((rows, 128), f32),
            pltpu.VMEM((128, 128), f32),
            pltpu.VMEM((blocks, half, 128), f32),
            pltpu.VMEM((blocks, rows, 128), f32),
            pltpu.VMEM((blocks, half, 128), f32),
            pltpu.VMEM((group, width), f32),
            pltpu.VMEM((feats, 1, 128), f32),
            dma((3,)),
            dma,
            dma,
            dma((tiles,)),
            dma((planes,)),
            dma,
            dma,
            dma((2 * planes,)),
            dma((2, tiles)),
            dma((chunks,)),
            dma((chunks,)),
            dma((chunks,)),
            dma((chunks,)),
            dma((feats,)),
            dma((feats,)),
        ],
        compiler_params=pltpu.CompilerParams(collective_id=0, has_side_effects=True),
    )(samples, start_vectors)


def solution(mesh, sub=SUB, planes=16, highs=2, lows=8):
    in_specs = (P(None, None, "feat"), P("comp", "feat"))
    return jax.shard_map(
        functools.partial(step, planes, highs, lows, sub),
        mesh=mesh,
        in_specs=in_specs,
        out_specs=P("comp", "feat"),
        check_vma=False,
    )
```

time: 1030 us -> 70.6 us (0.07)
  the two profiles are of different devices: /device:TPU:32 before, /device:TPU:224 now
where the time goes in v1:
time: 70.6 us; the launch traced here: 70.4 us
  Pallas kernels  68.8 us (97%)
  local copies, waits for them, and re-layouts  1.64 us (2%)
    pallas_call x1, Pallas kernels, step(): pl.pallas_call(functools.partial(kernel, planes, highs, lows, sub, width...  68.8 us
    unnamed x1, local copies, waits for them, and re-layouts  1.64 us

profile of v1, /device:TPU:224, one launch (start us, length us, event | category | flops | bytes accessed | tf_op | source)
XLA Modules:
  0.0 70.4 jit_solution(17257105028687144876)
XLA Ops:
  0.0 68.8 %shard_map.28 = f32[64,896]{1,0:T(8,128)} custom-call(f32[1,192,896]{2,1,0:T(8,128)} %s_hbm.1, f32[64,896]{1,0:T(8,128)} %u_hbm.1), custom_call_target="tpu_custom_call" | custom-call | tf_op jit(solution)/shard_map/pallas_call | solution.py:417
  68.8 1.6 %copy.4 = f32[64,896]{1,0:T(8,128)} copy(f32[64,896]{1,0:T(8,128)} %shard_map.28) | data formatting | bytes 458752

commit v2 on v1

v2 whole, which is shorter than its diff:
```python
import functools
import math

import jax
import jax.numpy as jnp
from jax import lax
from jax.experimental import pallas as pl
from jax.experimental.pallas import tpu as pltpu
from jax.sharding import PartitionSpec as P

MESH = pl.DeviceIdType.MESH
step_rate = 0.1
epsilon = 1e-06
highest = lax.Precision.HIGHEST

GEOMETRY = dict(planes=16, highs=2, lows=8)
SUB = 24


def dot(a, b, ca, cb):
    return lax.dot_general(
        a, b, (((ca,), (cb,)), ((), ())), precision=highest, preferred_element_type=jnp.float32
    )


def landed(ref, sem):
    pltpu.make_async_copy(ref, ref, sem).wait()


def kernel(
    planes, highs, lows, sub, features,
    s_hbm, u_hbm, out_hbm, scale_ref,
    new_v, s_v, u_pad, u_set, p_v, rs_v, zs_v, zr_v, tot_v, x_v, v_v, xt_v, xtt_v, own_v, in_v, o_v, fin_v,
    ld_sem, ux_send, ux_recv, rs_send, rs_recv, z_send, z_recv, ag_send, ag_recv,
    ch_send, lf_send, ch_recv, rl_send, rl_recv, fin_send, fin_recv, ready,
):
    rows, width = s_v.shape
    half = rows // 2
    tiles = half // 8 + 1
    group = 64
    blocks = width // 128
    subs = half // sub
    feats = planes * highs
    root = math.sqrt(features)

    comp = lax.axis_index("comp")
    feat = lax.axis_index("feat")
    core = lax.rem(comp, 2)
    low = lax.div(comp, 2)
    side = lax.rem(low, 2)
    high = lax.rem(feat, highs)
    plane = lax.div(feat, highs)
    partner = (low * 2 + 1 - core, feat)
    odd = side == 1
    even = side == 0
    fed = low >= 2
    forwards = jnp.logical_and(odd, low < lows - 2)
    mine = plane < tiles
    my_rows = pl.multiple_of(core * half, 8)
    other_feat = plane * highs + 1 - high

    load_s = pltpu.make_async_copy(s_hbm.at[0], s_v, ld_sem.at[0])
    load_u = pltpu.make_async_copy(u_hbm, u_pad.at[pl.ds(group, group)], ld_sem.at[1])

    def set_rows(side_, core_):
        return pl.ds(pl.multiple_of((side_ * 2 + core_) * group, 8), group)

    own_group = set_rows(side, core)
    load_c = pltpu.make_async_copy(u_hbm, u_set.at[own_group], ld_sem.at[2])
    load_u.start()
    load_s.start()
    load_c.start()

    barrier = pltpu.get_barrier_semaphore()

    def plane_peer(d):
        q = lax.rem(plane * 2 + core + d, 2 * planes)
        p = lax.div(q, 2)
        return low * 2 + lax.rem(q, 2), p * highs + high

    def greet(d, carry):
        pl.semaphore_signal(barrier, inc=1, device_id=plane_peer(d), device_id_type=MESH)
        return carry

    across = (comp, other_feat)
    right = (comp + 2, feat)
    right_across = (comp + 2, other_feat)
    left = (comp - 2, feat)
    ahead = (comp + 4, feat)
    behind = (comp - 4, feat)
    line = highs * lows

    def along(d):
        z = lax.rem(high * lows + low + d + line, line)
        return lax.rem(z, lows) * 2 + core, plane * highs + lax.div(z, lows)

    def signal(semaphore, device):
        pl.semaphore_signal(semaphore, inc=1, device_id=device, device_id_type=MESH)

    signal(barrier, along(lows // 2))
    signal(barrier, along(-(lows // 2)))

    @pl.when(even)
    def _():
        signal(barrier, right)

    @pl.when(odd)
    def _():
        signal(barrier, along(lows // 2 - 1))
        signal(barrier, along(-(lows // 2) - 1))
        signal(barrier, left)

        @pl.when(fed)
        def _():
            pl.semaphore_signal(barrier, inc=1, device_id=behind, device_id_type=MESH)

    lax.fori_loop(1, 2 * planes, greet, 0)

    u_pad[0:group, :] = jnp.zeros((group, width), jnp.float32)
    u_pad[2 * group : 3 * group, :] = jnp.zeros((group, width), jnp.float32)
    load_u.wait()
    u_own = u_pad[group : 2 * group, :]
    squares = jnp.zeros((group, 128), jnp.float32)
    for b in range(blocks):
        piece = u_own[:, b * 128 : (b + 1) * 128]
        squares = squares + piece * piece
    squares = jnp.concatenate([squares, squares], axis=0)
    p_v[tiles - 1] = dot(jnp.ones((8, 128), jnp.float32), squares, 1, 1)
    load_s.wait()
    projected = dot(s_v[0:half, :], u_pad[group : 3 * group, :], 1, 1) + dot(
        s_v[half:rows, :], u_pad[0 : 2 * group, :], 1, 1
    )
    for t in range(tiles - 1):
        p_v[t] = projected[8 * t : 8 * t + 8, :]

    pl.semaphore_wait(
        barrier,
        2 * planes
        + jnp.where(even, 4, 2).astype(jnp.int32)
        + jnp.where(forwards, 1, 0).astype(jnp.int32),
    )

    signal(ready, along(lows // 2))
    signal(ready, along(-(lows // 2)))

    def scatter(t, wait):
        copy = pltpu.make_async_remote_copy(
            src_ref=p_v.at[t],
            dst_ref=rs_v.at[plane],
            send_sem=rs_send.at[t],
            recv_sem=rs_recv.at[plane],
            device_id=(comp, t * highs + high),
            device_id_type=MESH,
        )

        @pl.when(t != plane)
        def _():
            if wait:
                copy.wait_send()
            else:
                copy.start()

    def scatter_start(t, carry):
        scatter(t, False)
        return carry

    lax.fori_loop(0, tiles, scatter_start, 0)

    def lend(side_, core_, slot, device):
        where = set_rows(side_, core_)
        return pltpu.make_async_remote_copy(
            src_ref=u_set.at[where],
            dst_ref=u_set.at[where],
            send_sem=ux_send.at[slot],
            recv_sem=ux_recv.at[side_, core_],
            device_id=device,
            device_id_type=MESH,
        )

    def borrowed(side_, core_):
        landed(u_set.at[set_rows(side_, core_)], ux_recv.at[side_, core_])

    load_c.wait()
    lend(side, core, 0, partner).start()

    @pl.when(even)
    def _():
        lend(side, core, 1, right).start()

    def exchange(slot, device):
        return pltpu.make_async_remote_copy(
            src_ref=zs_v,
            dst_ref=zr_v.at[side, high],
            send_sem=z_send.at[slot],
            recv_sem=z_recv.at[side, high],
            device_id=device,
            device_id_type=MESH,
        )

    def crossed(side_, high_):
        landed(zr_v.at[side_, high_], z_recv.at[side_, high_])

    def spread(side_, d):
        return pltpu.make_async_remote_copy(
            src_ref=tot_v.at[side_],
            dst_ref=x_v.at[side_, core, plane],
            send_sem=ag_send.at[side_, d],
            recv_sem=ag_recv.at[side_, core, plane],
            device_id=plane_peer(d),
            device_id_type=MESH,
        )

    @pl.when(mine)
    def _():
        rs_v[plane] = p_v[plane]
        pl.semaphore_wait(ready, 2)

        def arrive(p, carry):
            @pl.when(p != plane)
            def _():
                landed(rs_v.at[p], rs_recv.at[p])

            return carry

        lax.fori_loop(0, planes, arrive, 0)
        total = rs_v[0]
        for p in range(1, planes):
            total = total + rs_v[p]
        zs_v[...] = total
        exchange(0, across).start()

        @pl.when(even)
        def _():
            exchange(1, right_across).start()
            exchange(2, right).start()

        zr_v[side, high] = total

    @pl.when(jnp.logical_not(mine))
    def _():
        pl.semaphore_wait(ready, 2)

    @pl.when(odd)
    def _():
        borrowed(0, core)
        lend(0, core, 1, partner).start()

    def spread_side(side_):
        tot_v[side_] = zr_v[side_, 0] + zr_v[side_, 1]

        def spread_start(d, carry):
            spread(side_, d).start()
            return carry

        lax.fori_loop(1, 2 * planes, spread_start, 0)
        x_v[side_, core, plane] = zr_v[side_, 0] + zr_v[side_, 1]

    @pl.when(mine)
    def _():
        crossed(side, 1 - high)
        spread_side(side)

        @pl.when(odd)
        def _():
            crossed(0, 0)
            crossed(0, 1)
            spread_side(0)

    borrowed(side, 1 - core)

    @pl.when(odd)
    def _():
        borrowed(0, 1 - core)

    def gather_side(side_):
        def gathered(i, carry):
            g = lax.div(i, tiles)
            t = lax.rem(i, tiles)

            @pl.when(jnp.logical_or(g != core, t != plane))
            def _():
                landed(x_v.at[side_, g, t], ag_recv.at[side_, g, t])

            return carry

        lax.fori_loop(0, 2 * tiles, gathered, 0)

    lane = lax.broadcasted_iota(jnp.int32, (8, 128), 1)
    eye = lax.broadcasted_iota(jnp.int32, (128, 128), 0) == lax.broadcasted_iota(jnp.int32, (128, 128), 1)

    def prepare(side_):
        gather_side(side_)
        scale0 = lax.rsqrt(x_v[side_, 0, tiles - 1] / features + epsilon)
        scale1 = lax.rsqrt(x_v[side_, 1, tiles - 1] / features + epsilon)
        scale_row = jnp.where(lane < group, scale0, scale1)
        for t in range(tiles - 1):
            x0 = x_v[side_, 0, t] * scale0 / root
            x1 = x_v[side_, 1, t] * scale1 / root
            a = jnp.where(lane < group, x0, pltpu.roll(x1, 64, 1))
            b = jnp.where(lane < group, pltpu.roll(x0, 64, 1), x1)
            xt_v[side_, pl.ds(8 * t, 8), :] = a
            xt_v[side_, pl.ds(half + 8 * t, 8), :] = b
        scale_col = jnp.sum(
            jnp.where(eye, jnp.broadcast_to(scale_row[0:1, :], (128, 128)), 0.0), axis=1, keepdims=True
        )
        v_v[side_] = u_set[128 * side_ : 128 * side_ + 128, :] * scale_col

    @pl.when(odd)
    def _():
        prepare(1)

    prepare(0)

    def add_own(b):
        columns = pl.ds(pl.multiple_of(b * 128, 128), 128)
        here = pl.ds(my_rows, half)
        own_v[b] = dot(xt_v[0, here, :], v_v[0, :, columns], 1, 0) + dot(
            xt_v[1, here, :], v_v[1, :, columns], 1, 0
        )

    @pl.when(jnp.logical_and(forwards, fed))
    def _():
        def each(b, carry):
            add_own(b)
            return carry

        lax.fori_loop(0, blocks, each, 0)

    my_group = pl.ds(pl.multiple_of(core * group, 8), group)

    def base():
        x_own = xt_v[side]
        xtt_v[...] = x_own.T
        x_mine = xtt_v[my_group, :]
        i = lax.broadcasted_iota(jnp.int32, (group, 128), 0) + core * group
        j = lax.broadcasted_iota(jnp.int32, (group, 128), 1)
        pairs = jnp.where(j < i, dot(x_mine, x_own, 1, 0) / rows, 0.0)
        pull = dot(x_mine, s_v[...], 1, 0) * (root / rows) - dot(pairs, v_v[side], 1, 0)
        new_v[...] = v_v[side, my_group, :] + step_rate * pull

        @pl.when(odd)
        def _():
            cross = dot(x_mine, xt_v[0], 1, 0) / rows
            new_v[...] = new_v[...] - step_rate * dot(cross, v_v[0], 1, 0)

    starts = low == 1

    @pl.when(jnp.logical_not(starts))
    def _():
        base()

    def hop(b, s):
        i = b * subs + s
        here = pl.ds(pl.multiple_of(my_rows + s * sub, 8), sub)
        there = pl.ds(pl.multiple_of(s * sub, 8), sub)

        def send(src, sem, arrival, device):
            return pltpu.make_async_remote_copy(
                src_ref=src,
                dst_ref=in_v.at[b, here],
                send_sem=sem.at[i],
                recv_sem=arrival.at[i],
                device_id=device,
                device_id_type=MESH,
            )

        forward = send(o_v.at[b, there], ch_send, ch_recv, ahead)
        back = send(in_v.at[b, here], lf_send, ch_recv, left)
        relay = send(in_v.at[b, here], rl_send, rl_recv, partner)
        return here, there, forward, back, relay

    def finish(b):
        def arrived(s, carry):
            other = pl.ds(pl.multiple_of((1 - core) * half + s * sub, 8), sub)
            landed(in_v.at[b, other], rl_recv.at[b * subs + s])
            return carry

        lax.fori_loop(0, subs, arrived, 0)
        columns = pl.ds(pl.multiple_of(b * 128, 128), 128)
        new_v[:, columns] = new_v[:, columns] - dot(xtt_v[my_group, :], in_v[b], 1, 0) * (step_rate / rows)

    def chain(b, carry):
        @pl.when(starts)
        def _():
            add_own(b)

        def one(s, carry):
            here, there, forward, back, relay = hop(b, s)

            @pl.when(fed)
            def _():
                landed(in_v.at[b, here], ch_recv.at[b * subs + s])

                @pl.when(forwards)
                def _():
                    o_v[b, there] = in_v[b, here] + own_v[b, there]
                    forward.start()

                @pl.when(odd)
                def _():
                    back.start()

                relay.start()

            @pl.when(starts)
            def _():
                o_v[b, there] = own_v[b, there]
                forward.start()

            return carry

        lax.fori_loop(0, subs, one, 0)

        @pl.when(jnp.logical_and(jnp.logical_and(fed, jnp.logical_not(forwards)), b > 0))
        def _():
            finish(b - 1)

        return carry

    lax.fori_loop(0, blocks, chain, 0)

    @pl.when(jnp.logical_and(fed, jnp.logical_not(forwards)))
    def _():
        finish(blocks - 1)

    @pl.when(starts)
    def _():
        base()

    @pl.when(jnp.logical_and(fed, forwards))
    def _():
        def finish_all(b, carry):
            finish(b)
            return carry

        lax.fori_loop(0, blocks, finish_all, 0)

    squares = jnp.zeros((group, 128), jnp.float32)
    for b in range(blocks):
        piece = new_v[:, b * 128 : (b + 1) * 128]
        squares = squares + piece * piece
    column = jnp.sum(squares, axis=1, keepdims=True)
    eye_half = lax.broadcasted_iota(jnp.int32, (group, 128), 0) == lax.broadcasted_iota(
        jnp.int32, (group, 128), 1
    )
    fin_v[feat] = jnp.sum(jnp.where(eye_half, column, 0.0), axis=0, keepdims=True)

    def tell(d):
        q = lax.rem(feat + d, feats)
        return pltpu.make_async_remote_copy(
            src_ref=fin_v.at[feat],
            dst_ref=fin_v.at[feat],
            send_sem=fin_send.at[d],
            recv_sem=fin_recv.at[feat],
            device_id=(comp, q),
            device_id_type=MESH,
        )

    def tell_start(d, carry):
        tell(d).start()
        return carry

    lax.fori_loop(1, feats, tell_start, 0)
    store = pltpu.make_async_copy(new_v, out_hbm, ld_sem.at[0])
    store.start()

    def scatter_end(t, carry):
        scatter(t, True)
        return carry

    lax.fori_loop(0, tiles, scatter_end, 0)
    lend(side, core, 0, partner).wait_send()

    @pl.when(even)
    def _():
        lend(side, core, 1, right).wait_send()

    @pl.when(odd)
    def _():
        lend(0, core, 1, partner).wait_send()

    def spread_end_of(side_):
        def spread_end(d, carry):
            spread(side_, d).wait_send()
            return carry

        lax.fori_loop(1, 2 * planes, spread_end, 0)

    @pl.when(mine)
    def _():
        exchange(0, across).wait_send()

        @pl.when(even)
        def _():
            exchange(1, right_across).wait_send()
            exchange(2, right).wait_send()

        spread_end_of(side)

        @pl.when(odd)
        def _():
            spread_end_of(0)

    def chain_end(i, carry):
        here, there, forward, back, relay = hop(lax.div(i, subs), lax.rem(i, subs))

        @pl.when(forwards)
        def _():
            forward.wait_send()

        @pl.when(fed)
        def _():
            relay.wait_send()

            @pl.when(odd)
            def _():
                back.wait_send()

        return carry

    lax.fori_loop(0, blocks * subs, chain_end, 0)

    def told(d, carry):
        q = lax.rem(feat + d, feats)
        landed(fin_v.at[q], fin_recv.at[q])
        return carry

    lax.fori_loop(1, feats, told, 0)
    total = fin_v[0]
    for q in range(1, feats):
        total = total + fin_v[q]
    scale_ref[...] = jnp.broadcast_to(
        lax.rsqrt(
            jnp.sum(jnp.where(eye_half, jnp.broadcast_to(total, (group, 128)), 0.0), axis=1, keepdims=True)
            / features
            + epsilon
        ),
        (group, width),
    )

    def tell_end(d, carry):
        tell(d).wait_send()
        return carry

    lax.fori_loop(1, feats, tell_end, 0)
    store.wait()


def step(planes, highs, lows, sub, samples, start_vectors):
    _, rows, width = samples.shape
    group = start_vectors.shape[0]
    feats = planes * highs
    half = rows // 2
    tiles = half // 8 + 1
    blocks = width // 128
    chunks = blocks * (half // sub)
    dma = pltpu.SemaphoreType.DMA
    f32 = jnp.float32
    updated, scale = pl.pallas_call(
        functools.partial(kernel, planes, highs, lows, sub, width * feats),
        out_shape=(
            jax.ShapeDtypeStruct((group, width), f32),
            jax.ShapeDtypeStruct((group, width), f32),
        ),
        in_specs=[pl.BlockSpec(memory_space=pl.ANY)] * 2,
        out_specs=(pl.BlockSpec(memory_space=pl.ANY), pl.BlockSpec(memory_space=pltpu.VMEM)),
        scratch_shapes=[
            pltpu.VMEM((group, width), f32),
            pltpu.VMEM((rows, width), f32),
            pltpu.VMEM((3 * group, width), f32),
            pltpu.VMEM((4 * group, width), f32),
            pltpu.VMEM((tiles, 8, 128), f32),
            pltpu.VMEM((planes, 8, 128), f32),
            pltpu.VMEM((8, 128), f32),
            pltpu.VMEM((2, 2, 8, 128), f32),
            pltpu.VMEM((2, 8, 128), f32),
            pltpu.VMEM((2, 2, tiles, 8, 128), f32),
            pltpu.VMEM((2, 2 * group, width), f32),
            pltpu.VMEM((2, rows, 128), f32),
            pltpu.VMEM((128, rows), f32),
            pltpu.VMEM((blocks, half, 128), f32),
            pltpu.VMEM((blocks, rows, 128), f32),
            pltpu.VMEM((blocks, half, 128), f32),
            pltpu.VMEM((feats, 1, 128), f32),
            dma((3,)),
            dma((2,)),
            dma((2, 2)),
            dma((tiles,)),
            dma((planes,)),
            dma((3,)),
            dma((2, 2)),
            dma((2, 2 * planes)),
            dma((2, 2, tiles)),
            dma((chunks,)),
            dma((chunks,)),
            dma((chunks,)),
            dma((chunks,)),
            dma((chunks,)),
            dma((feats,)),
            dma((feats,)),
            pltpu.SemaphoreType.REGULAR,
        ],
        compiler_params=pltpu.CompilerParams(collective_id=0, has_side_effects=True, vmem_limit_bytes=54700 * 1024),
    )(samples, start_vectors)
    return updated * scale


def solution(mesh, sub=SUB, planes=16, highs=2, lows=8):
    in_specs = (P(None, None, "feat"), P("comp", "feat"))
    return jax.shard_map(
        functools.partial(step, planes, highs, lows, sub),
        mesh=mesh,
        in_specs=in_specs,
        out_specs=P("comp", "feat"),
        check_vma=False,
    )
```

time: 70.6 us -> 61.2 us (0.87)
  the two profiles are of different devices: /device:TPU:224 before, /device:TPU:193 now
where the time goes in v2:
time: 61.2 us; the launch traced here: 61.1 us
  Pallas kernels  60.4 us (99%)
  other arithmetic  0.71 us (1%)
    pallas_call x1, Pallas kernels, step(): pl.pallas_call(functools.partial(kernel, planes, highs, lows, sub, width...  60.4 us

profile of v2, /device:TPU:193, one launch (start us, length us, event | category | flops | bytes accessed | tf_op | source)
XLA Modules:
  0.0 61.1 jit_solution(1607029728622323398)
XLA Ops:
  0.0 60.4 %shard_map.28 = (f32[64,896]{1,0:T(8,128)S(1)}, f32[64,896]{1,0:T(8,128)S(1)}) custom-call(f32[1,192,896]{2,1,0:T(8,128)} %s_hbm.1, f32[64,896]{1,0:T(8,128)} %u_hbm.1), custom_call_target="tpu_custom_call" | custom-call | tf_op jit(solution)/shard_map/pallas_call | solution.py:559
  60.4 0.7 %mul.3 = f32[64,896]{1,0:T(8,128)} multiply(f32[64,896]{1,0:T(8,128)S(1)} %get-tuple-element.7, f32[64,896]{1,0:T(8,128)S(1)} %get-tuple-element.8) | non-fusion elementwise | flops 57344 | bytes 688128 | tf_op jit(solution)/shard_map/mul | solution.py:605

commit v3 on v2

v3 whole, which is shorter than its diff:
```python
import functools
import math

import jax
import jax.numpy as jnp
from jax import lax
from jax.experimental import pallas as pl
from jax.experimental.pallas import tpu as pltpu
from jax.sharding import PartitionSpec as P

MESH = pl.DeviceIdType.MESH
step_rate = 0.1
epsilon = 1e-06
highest = lax.Precision.HIGHEST

SUB = 24
OWNERS = (2, 2, 8, 8, 5, 7, 13, 15, 1, 3, 4, 12, 0)


def dot(a, b, ca, cb):
    return lax.dot_general(
        a, b, (((ca,), (cb,)), ((), ())), precision=highest, preferred_element_type=jnp.float32
    )


def landed(ref, sem):
    pltpu.make_async_copy(ref, ref, sem).wait()


def kernel(
    planes, highs, lows, sub, owners, features,
    s_hbm, u_hbm, out_hbm, scale_ref,
    new_v, s_v, u_pad, u_set, p_v, rs_v, zs_v, zr_v, tot_v, x_v, v_v, xt_v, xtt_v, own_v, in_v, o_v, fin_v, sent_v,
    ld_sem, ux_send, ux_recv, rs_send, rs_recv, z_send, z_recv, ag_send, ag_recv, xr_send, xr_recv,
    ch_send, lf_send, ch_recv, rl_send, rl_recv, fin_send, fin_recv, ready,
):
    rows, width = s_v.shape
    half = rows // 2
    tiles = half // 8 + 1
    group = 64
    blocks = width // 128
    subs = half // sub
    feats = planes * highs
    root = math.sqrt(features)

    comp = lax.axis_index("comp")
    feat = lax.axis_index("feat")
    core = lax.rem(comp, 2)
    low = lax.div(comp, 2)
    side = lax.rem(low, 2)
    high = lax.rem(feat, highs)
    plane = lax.div(feat, highs)
    partner = (low * 2 + 1 - core, feat)
    odd = side == 1
    even = side == 0
    fed = low >= 2
    single = low >= lows - 2
    forwards = jnp.logical_or(jnp.logical_and(odd, jnp.logical_not(single)), low == lows - 2)
    lends = jnp.logical_and(even, jnp.logical_not(single))
    heads = jnp.logical_and(odd, jnp.logical_not(single))
    slot_of = [owners[:t].count(owners[t]) for t in range(tiles)]
    slots = max(slot_of) + 1
    first_tile, count = 0, 0
    for t in range(tiles):
        owned = plane == owners[t]
        count = count + jnp.where(owned, 1, 0).astype(jnp.int32)
        if slot_of[t] == 0:
            first_tile = first_tile + jnp.where(owned, t, 0).astype(jnp.int32)
    side_len = math.isqrt(planes)
    reach = side_len // 2
    here_x = lax.div(plane, side_len)
    here_y = lax.rem(plane, side_len)

    def plane_at(k):
        x = lax.rem(here_x + reach + lax.div(k, side_len), side_len)
        y = lax.rem(here_y + reach + lax.rem(k, side_len), side_len)
        return x * side_len + y

    itself = reach * side_len + reach
    my_rows = pl.multiple_of(core * half, 8)
    other_feat = plane * highs + 1 - high

    load_s = pltpu.make_async_copy(s_hbm.at[0], s_v, ld_sem.at[0])
    load_u = pltpu.make_async_copy(u_hbm, u_pad.at[pl.ds(group, group)], ld_sem.at[1])

    def set_rows(side_, core_):
        return pl.ds(pl.multiple_of((side_ * 2 + core_) * group, 8), group)

    own_group = set_rows(side, core)
    load_c = pltpu.make_async_copy(u_hbm, u_set.at[own_group], ld_sem.at[2])
    load_u.start()
    load_s.start()
    load_c.start()

    barrier = pltpu.get_barrier_semaphore()

    def plane_peer(d):
        q = lax.rem(plane * 2 + core + d, 2 * planes)
        p = lax.div(q, 2)
        return low * 2 + lax.rem(q, 2), p * highs + high

    def greet(d, carry):
        pl.semaphore_signal(barrier, inc=1, device_id=plane_peer(d), device_id_type=MESH)
        return carry

    across = (comp, other_feat)
    right = (comp + 2, feat)
    right_across = (comp + 2, other_feat)
    left = (comp - 2, feat)
    ahead = (comp + 4, feat)
    behind = (comp - 4, feat)
    line = highs * lows

    def along(d):
        z = lax.rem(high * lows + low + d + line, line)
        return lax.rem(z, lows) * 2 + core, plane * highs + lax.div(z, lows)

    def signal(semaphore, device):
        pl.semaphore_signal(semaphore, inc=1, device_id=device, device_id_type=MESH)

    signal(barrier, along(lows // 2))
    signal(barrier, along(-(lows // 2)))

    @pl.when(even)
    def _():
        signal(barrier, right)

    @pl.when(odd)
    def _():
        signal(barrier, along(lows // 2 - 1))
        signal(barrier, along(-(lows // 2) - 1))
        signal(barrier, left)

        @pl.when(jnp.logical_and(fed, heads))
        def _():
            signal(barrier, behind)

    @pl.when(low == lows - 2)
    def _():
        signal(barrier, left)

    lax.fori_loop(1, 2 * planes, greet, 0)

    u_pad[0:group, :] = jnp.zeros((group, width), jnp.float32)
    u_pad[2 * group : 3 * group, :] = jnp.zeros((group, width), jnp.float32)
    load_u.wait()
    u_own = u_pad[group : 2 * group, :]
    squares = jnp.zeros((group, 128), jnp.float32)
    for b in range(blocks):
        piece = u_own[:, b * 128 : (b + 1) * 128]
        squares = squares + piece * piece
    squares = jnp.concatenate([squares, squares], axis=0)
    p_v[tiles - 1] = dot(jnp.ones((8, 128), jnp.float32), squares, 1, 1)
    load_s.wait()
    projected = dot(s_v[0:half, :], u_pad[group : 3 * group, :], 1, 1) + dot(
        s_v[half:rows, :], u_pad[0 : 2 * group, :], 1, 1
    )
    for t in range(tiles - 1):
        p_v[t] = projected[8 * t : 8 * t + 8, :]

    pl.semaphore_wait(
        barrier,
        2 * planes
        + jnp.where(even, 4, 2).astype(jnp.int32)
        + jnp.where(heads, 1, 0).astype(jnp.int32),
    )

    signal(ready, along(lows // 2))
    signal(ready, along(-(lows // 2)))

    for t in range(tiles):

        @pl.when(plane != owners[t])
        def _():
            pltpu.make_async_remote_copy(
                src_ref=p_v.at[t],
                dst_ref=rs_v.at[slot_of[t], plane],
                send_sem=rs_send,
                recv_sem=rs_recv,
                device_id=(comp, owners[t] * highs + high),
                device_id_type=MESH,
            ).start()

    def lend(side_, core_, slot, device):
        where = set_rows(side_, core_)
        return pltpu.make_async_remote_copy(
            src_ref=u_set.at[where],
            dst_ref=u_set.at[where],
            send_sem=ux_send.at[slot],
            recv_sem=ux_recv.at[side_, core_],
            device_id=device,
            device_id_type=MESH,
        )

    def borrowed(side_, core_):
        landed(u_set.at[set_rows(side_, core_)], ux_recv.at[side_, core_])

    load_c.wait()
    lend(side, core, 0, partner).start()

    @pl.when(lends)
    def _():
        lend(side, core, 1, right).start()

    def exchange(n, device):
        return pltpu.make_async_remote_copy(
            src_ref=zs_v.at[pl.ds(0, n)],
            dst_ref=zr_v.at[side, high, pl.ds(0, n)],
            send_sem=z_send,
            recv_sem=z_recv.at[side, high],
            device_id=device,
            device_id_type=MESH,
        )

    def crossed(n, side_, high_):
        landed(zr_v.at[side_, high_, pl.ds(0, n)], z_recv.at[side_, high_])

    pl.semaphore_wait(ready, 2)
    for n in range(1, slots + 1):

        @pl.when(count == n)
        def _():
            for slot in range(n):
                rs_v[slot, plane] = p_v[first_tile + slot]
            landed(rs_v.at[pl.ds(0, n), pl.ds(0, planes - 1)], rs_recv)
            for slot in range(n):
                total = rs_v[slot, 0]
                for p in range(1, planes):
                    total = total + rs_v[slot, p]
                zs_v[slot] = total
            exchange(n, across).start()

            @pl.when(lends)
            def _():
                exchange(n, right_across).start()
                exchange(n, right).start()

            for slot in range(n):
                zr_v[side, high, slot] = zs_v[slot]

    @pl.when(heads)
    def _():
        borrowed(0, core)
        lend(0, core, 1, partner).start()

    place = core * tiles + first_tile

    def spread_side(n, side_):
        for slot in range(n):
            total = zr_v[side_, 0, slot] + zr_v[side_, 1, slot]
            tot_v[side_, slot] = total
            x_v[side_, place + slot] = total

        def spread_start(k, carry):
            @pl.when(k != itself)
            def _():
                pltpu.make_async_remote_copy(
                    src_ref=tot_v.at[side_, pl.ds(0, n)],
                    dst_ref=x_v.at[side_, pl.ds(place, n)],
                    send_sem=ag_send.at[side_],
                    recv_sem=ag_recv.at[side_],
                    device_id=(comp, plane_at(k) * highs + high),
                    device_id_type=MESH,
                ).start()

            return carry

        lax.fori_loop(0, planes, spread_start, 0)

    for n in range(1, slots + 1):

        @pl.when(count == n)
        def _():
            crossed(n, side, 1 - high)
            spread_side(n, side)

            @pl.when(heads)
            def _():
                crossed(n, 0, 0)
                crossed(n, 0, 1)
                spread_side(n, 0)

    borrowed(side, 1 - core)

    @pl.when(heads)
    def _():
        borrowed(0, 1 - core)

    def pass_on(side_):
        tiles_here = pl.ds(core * tiles, tiles)
        return pltpu.make_async_remote_copy(
            src_ref=x_v.at[side_, tiles_here],
            dst_ref=x_v.at[side_, tiles_here],
            send_sem=xr_send.at[side_],
            recv_sem=xr_recv.at[side_],
            device_id=partner,
            device_id_type=MESH,
        )

    def collect(side_):
        for n in range(slots + 1):

            @pl.when(count == n)
            def _():
                landed(x_v.at[side_, pl.ds(0, tiles - n)], ag_recv.at[side_])

        pass_on(side_).start()

    collect(side)

    @pl.when(heads)
    def _():
        collect(0)

    def gather_side(side_):
        landed(x_v.at[side_, pl.ds((1 - core) * tiles, tiles)], xr_recv.at[side_])

    lane = lax.broadcasted_iota(jnp.int32, (8, 128), 1)
    eye = lax.broadcasted_iota(jnp.int32, (128, 128), 0) == lax.broadcasted_iota(jnp.int32, (128, 128), 1)

    def prepare(side_):
        gather_side(side_)
        scale0 = lax.rsqrt(x_v[side_, tiles - 1] / features + epsilon)
        scale1 = lax.rsqrt(x_v[side_, 2 * tiles - 1] / features + epsilon)
        scale_row = jnp.where(lane < group, scale0, scale1)
        for t in range(tiles - 1):
            x0 = x_v[side_, t] * scale0 / root
            x1 = x_v[side_, tiles + t] * scale1 / root
            a = jnp.where(lane < group, x0, pltpu.roll(x1, 64, 1))
            b = jnp.where(lane < group, pltpu.roll(x0, 64, 1), x1)
            xt_v[side_, pl.ds(8 * t, 8), :] = a
            xt_v[side_, pl.ds(half + 8 * t, 8), :] = b
        scale_col = jnp.sum(
            jnp.where(eye, jnp.broadcast_to(scale_row[0:1, :], (128, 128)), 0.0), axis=1, keepdims=True
        )
        v_v[side_] = u_set[128 * side_ : 128 * side_ + 128, :] * scale_col

    @pl.when(odd)
    def _():
        prepare(1)

    @pl.when(jnp.logical_or(even, heads))
    def _():
        prepare(0)

    def add_own(b):
        columns = pl.ds(pl.multiple_of(b * 128, 128), 128)
        here = pl.ds(my_rows, half)
        own_v[b] = dot(xt_v[0, here, :], v_v[0, :, columns], 1, 0)

        @pl.when(heads)
        def _():
            own_v[b] = own_v[b] + dot(xt_v[1, here, :], v_v[1, :, columns], 1, 0)

    @pl.when(jnp.logical_and(forwards, fed))
    def _():
        def each(b, carry):
            add_own(b)
            return carry

        lax.fori_loop(0, blocks, each, 0)

    my_group = pl.ds(pl.multiple_of(core * group, 8), group)

    def base():
        x_own = xt_v[side]
        xtt_v[...] = x_own.T
        x_mine = xtt_v[my_group, :]
        i = lax.broadcasted_iota(jnp.int32, (group, 128), 0) + core * group
        j = lax.broadcasted_iota(jnp.int32, (group, 128), 1)
        pairs = jnp.where(j < i, dot(x_mine, x_own, 1, 0) / rows, 0.0)
        pull = dot(x_mine, s_v[...], 1, 0) * (root / rows) - dot(pairs, v_v[side], 1, 0)
        new_v[...] = v_v[side, my_group, :] + step_rate * pull

        @pl.when(heads)
        def _():
            cross = dot(x_mine, xt_v[0], 1, 0) / rows
            new_v[...] = new_v[...] - step_rate * dot(cross, v_v[0], 1, 0)

    starts = low == 1
    late = jnp.logical_and(heads, low < 5)

    @pl.when(jnp.logical_not(late))
    def _():
        base()

    def hop(b, s):
        i = b * subs + s
        here = pl.ds(pl.multiple_of(my_rows + s * sub, 8), sub)
        there = pl.ds(pl.multiple_of(s * sub, 8), sub)

        def send(src, sem, arrival, device):
            return pltpu.make_async_remote_copy(
                src_ref=src,
                dst_ref=in_v.at[b, here],
                send_sem=sem,
                recv_sem=arrival,
                device_id=device,
                device_id_type=MESH,
            )

        target = comp + jnp.where(low < lows - 3, 4, 2).astype(jnp.int32)
        forward = send(o_v.at[b, there], ch_send, ch_recv.at[i], (target, feat))
        back = send(in_v.at[b, here], lf_send, ch_recv.at[i], left)
        relay = send(in_v.at[b, here], rl_send, rl_recv.at[b], partner)
        return here, there, forward, back, relay

    def finish(b):
        other = pl.ds(pl.multiple_of((1 - core) * half, 8), half)
        landed(in_v.at[b, other], rl_recv.at[b])
        columns = pl.ds(pl.multiple_of(b * 128, 128), 128)
        new_v[:, columns] = new_v[:, columns] - dot(xtt_v[my_group, :], in_v[b], 1, 0) * (step_rate / rows)

    def chain(b, carry):
        @pl.when(starts)
        def _():
            add_own(b)

        def one(s, carry):
            here, there, forward, back, relay = hop(b, s)

            @pl.when(fed)
            def _():
                landed(in_v.at[b, here], ch_recv.at[b * subs + s])

                @pl.when(forwards)
                def _():
                    o_v[b, there] = in_v[b, here] + own_v[b, there]
                    forward.start()

                @pl.when(heads)
                def _():
                    back.start()

                relay.start()

            @pl.when(starts)
            def _():
                o_v[b, there] = own_v[b, there]
                forward.start()

            return carry

        lax.fori_loop(0, subs, one, 0)

        @pl.when(jnp.logical_and(jnp.logical_and(fed, jnp.logical_not(forwards)), b > 0))
        def _():
            finish(b - 1)

        return carry

    lax.fori_loop(0, blocks, chain, 0)

    @pl.when(jnp.logical_and(fed, jnp.logical_not(forwards)))
    def _():
        finish(blocks - 1)

    @pl.when(late)
    def _():
        base()

    @pl.when(jnp.logical_and(fed, forwards))
    def _():
        def finish_all(b, carry):
            finish(b)
            return carry

        lax.fori_loop(0, blocks, finish_all, 0)

    squares = jnp.zeros((group, 128), jnp.float32)
    for b in range(blocks):
        piece = new_v[:, b * 128 : (b + 1) * 128]
        squares = squares + piece * piece
    column = jnp.sum(squares, axis=1, keepdims=True)
    eye_half = lax.broadcasted_iota(jnp.int32, (group, 128), 0) == lax.broadcasted_iota(
        jnp.int32, (group, 128), 1
    )
    fin_v[feat] = jnp.sum(jnp.where(eye_half, column, 0.0), axis=0, keepdims=True)

    def tell(k, high_):
        pltpu.make_async_remote_copy(
            src_ref=fin_v.at[feat],
            dst_ref=fin_v.at[feat],
            send_sem=fin_send,
            recv_sem=fin_recv,
            device_id=(comp, plane_at(k) * highs + high_),
            device_id_type=MESH,
        ).start()

    def tell_across(k, carry):
        tell(k, 1 - high)
        return carry

    def tell_plane(k, carry):
        @pl.when(k != itself)
        def _():
            tell(k, high)

        return carry

    lax.fori_loop(0, planes, tell_across, 0)
    lax.fori_loop(0, planes, tell_plane, 0)
    store = pltpu.make_async_copy(new_v, out_hbm, ld_sem.at[0])
    store.start()

    for n in range(slots + 1):

        @pl.when(count == n)
        def _():
            landed(sent_v.at[pl.ds(0, tiles - n)], rs_send)

    lend(side, core, 0, partner).wait_send()

    @pl.when(lends)
    def _():
        lend(side, core, 1, right).wait_send()

    @pl.when(heads)
    def _():
        lend(0, core, 1, partner).wait_send()

    pass_on(side).wait_send()

    @pl.when(heads)
    def _():
        pass_on(0).wait_send()

    for n in range(1, slots + 1):

        @pl.when(count == n)
        def _():
            @pl.when(lends)
            def _():
                landed(sent_v.at[pl.ds(0, 3 * n)], z_send)

            @pl.when(jnp.logical_not(lends))
            def _():
                landed(sent_v.at[pl.ds(0, n)], z_send)

            landed(sent_v.at[pl.ds(0, n * (planes - 1))], ag_send.at[side])

            @pl.when(heads)
            def _():
                landed(sent_v.at[pl.ds(0, n * (planes - 1))], ag_send.at[0])

    @pl.when(forwards)
    def _():
        landed(o_v, ch_send)

    @pl.when(fed)
    def _():
        landed(o_v, rl_send)

        @pl.when(heads)
        def _():
            landed(o_v, lf_send)

    landed(fin_v.at[pl.ds(0, feats - 1)], fin_recv)
    total = fin_v[0]
    for q in range(1, feats):
        total = total + fin_v[q]
    scale_ref[...] = jnp.broadcast_to(
        lax.rsqrt(
            jnp.sum(jnp.where(eye_half, jnp.broadcast_to(total, (group, 128)), 0.0), axis=1, keepdims=True)
            / features
            + epsilon
        ),
        (group, width),
    )

    landed(fin_v.at[pl.ds(0, feats - 1)], fin_send)
    store.wait()


def step(planes, highs, lows, sub, owners, samples, start_vectors):
    _, rows, width = samples.shape
    group = start_vectors.shape[0]
    feats = planes * highs
    half = rows // 2
    tiles = half // 8 + 1
    blocks = width // 128
    chunks = blocks * (half // sub)
    slots = max(owners.count(plane) for plane in owners)
    dma = pltpu.SemaphoreType.DMA
    f32 = jnp.float32
    updated, scale = pl.pallas_call(
        functools.partial(kernel, planes, highs, lows, sub, owners, width * feats),
        out_shape=(
            jax.ShapeDtypeStruct((group, width), f32),
            jax.ShapeDtypeStruct((group, width), f32),
        ),
        in_specs=[pl.BlockSpec(memory_space=pl.ANY)] * 2,
        out_specs=(pl.BlockSpec(memory_space=pl.ANY), pl.BlockSpec(memory_space=pltpu.VMEM)),
        scratch_shapes=[
            pltpu.VMEM((group, width), f32),
            pltpu.VMEM((rows, width), f32),
            pltpu.VMEM((3 * group, width), f32),
            pltpu.VMEM((4 * group, width), f32),
            pltpu.VMEM((tiles, 8, 128), f32),
            pltpu.VMEM((slots, planes, 8, 128), f32),
            pltpu.VMEM((slots, 8, 128), f32),
            pltpu.VMEM((2, 2, slots, 8, 128), f32),
            pltpu.VMEM((2, slots, 8, 128), f32),
            pltpu.VMEM((2, 2 * tiles, 8, 128), f32),
            pltpu.VMEM((2, 2 * group, width), f32),
            pltpu.VMEM((2, rows, 128), f32),
            pltpu.VMEM((128, rows), f32),
            pltpu.VMEM((blocks, half, 128), f32),
            pltpu.VMEM((blocks, rows, 128), f32),
            pltpu.VMEM((blocks, half, 128), f32),
            pltpu.VMEM((feats, 1, 128), f32),
            pltpu.VMEM((slots * planes, 8, 128), f32),
            dma((3,)),
            dma((2,)),
            dma((2, 2)),
            dma,
            dma,
            dma,
            dma((2, 2)),
            dma((2,)),
            dma((2,)),
            dma((2,)),
            dma((2,)),
            dma,
            dma,
            dma((chunks,)),
            dma,
            dma((blocks,)),
            dma,
            dma,
            pltpu.SemaphoreType.REGULAR,
        ],
        compiler_params=pltpu.CompilerParams(collective_id=0, has_side_effects=True, vmem_limit_bytes=54700 * 1024),
    )(samples, start_vectors)
    return updated * scale


def solution(mesh, sub=SUB, owners=OWNERS, planes=16, highs=2, lows=8):
    in_specs = (P(None, None, "feat"), P("comp", "feat"))
    return jax.shard_map(
        functools.partial(step, planes, highs, lows, sub, owners),
        mesh=mesh,
        in_specs=in_specs,
        out_specs=P("comp", "feat"),
        check_vma=False,
    )
```

time: 61.2 us -> 56.1 us (0.917)
  the two profiles are of different devices: /device:TPU:193 before, /device:TPU:128 now
where the time goes in v3:
time: 56.1 us; the launch traced here: 56 us
  Pallas kernels  55.2 us (98%)
  other arithmetic  0.71 us (1%)
    pallas_call x1, Pallas kernels, step(): pl.pallas_call(functools.partial(kernel, planes, highs, lows, sub, owners...  55.2 us

profile of v3, /device:TPU:128, one launch (start us, length us, event | category | flops | bytes accessed | tf_op | source)
XLA Modules:
  0.0 56.0 jit_solution(10389715096974873862)
XLA Ops:
  0.0 55.2 %shard_map.28 = (f32[64,896]{1,0:T(8,128)S(1)}, f32[64,896]{1,0:T(8,128)S(1)}) custom-call(f32[1,192,896]{2,1,0:T(8,128)} %s_hbm.1, f32[64,896]{1,0:T(8,128)} %u_hbm.1), custom_call_target="tpu_custom_call" | custom-call | tf_op jit(solution)/shard_map/pallas_call | solution.py:586
  55.2 0.7 %mul.3 = f32[64,896]{1,0:T(8,128)} multiply(f32[64,896]{1,0:T(8,128)S(1)} %get-tuple-element.7, f32[64,896]{1,0:T(8,128)S(1)} %get-tuple-element.8) | non-fusion elementwise | flops 57344 | bytes 688128 | tf_op jit(solution)/shard_map/mul | solution.py:635

commit v4 on v3

--- a/solution.py
+++ b/solution.py
@@ -14,15 +14,30 @@
 highest = lax.Precision.HIGHEST
 
 SUB = 24
-OWNERS = (2, 2, 8, 8, 5, 7, 13, 15, 1, 3, 4, 12, 0)
-
-
-def dot(a, b, ca, cb):
+OWNERS = (10, 10, 6, 6, 9, 11, 14, 2, 5, 7, 8, 13, 15)
+
+
+def dot_exact(a, b, ca, cb):
     return lax.dot_general(
         a, b, (((ca,), (cb,)), ((), ())), precision=highest, preferred_element_type=jnp.float32
     )
 
 
+def split(a):
+    high = a.astype(jnp.bfloat16)
+    return high, (a - high.astype(jnp.float32)).astype(jnp.bfloat16)
+
+
+def dot(a, b, ca, cb):
+    a_high, a_low = split(a)
+    b_high, b_low = split(b)
+
+    def product(x, y):
+        return lax.dot_general(x, y, (((ca,), (cb,)), ((), ())), preferred_element_type=jnp.float32)
+
+    return product(a_high, b_high) + (product(a_high, b_low) + product(a_low, b_high))
+
+
 def landed(ref, sem):
     pltpu.make_async_copy(ref, ref, sem).wait()
 
@@ -30,7 +45,7 @@
 def kernel(
     planes, highs, lows, sub, owners, features,
     s_hbm, u_hbm, out_hbm, scale_ref,
-    new_v, s_v, u_pad, u_set, p_v, rs_v, zs_v, zr_v, tot_v, x_v, v_v, xt_v, xtt_v, own_v, in_v, o_v, fin_v, sent_v,
+    new_v, s_v, u_pad, u_set, p_v, rs_v, zs_v, zr_v, tot_v, x_v, v_v, xt_v, xs_v, xtt_v, own_v, in_v, o_v, fin_v, sent_v,
     ld_sem, ux_send, ux_recv, rs_send, rs_recv, z_send, z_recv, ag_send, ag_recv, xr_send, xr_recv,
     ch_send, lf_send, ch_recv, rl_send, rl_recv, fin_send, fin_recv, ready,
 ):
@@ -80,7 +95,10 @@
     my_rows = pl.multiple_of(core * half, 8)
     other_feat = plane * highs + 1 - high
 
-    load_s = pltpu.make_async_copy(s_hbm.at[0], s_v, ld_sem.at[0])
+    load_s = [
+        pltpu.make_async_copy(s_hbm.at[0, pl.ds(r, half)], s_v.at[pl.ds(r, half)], ld_sem.at[n])
+        for n, r in ((0, 0), (3, half))
+    ]
     load_u = pltpu.make_async_copy(u_hbm, u_pad.at[pl.ds(group, group)], ld_sem.at[1])
 
     def set_rows(side_, core_):
@@ -89,19 +107,11 @@
     own_group = set_rows(side, core)
     load_c = pltpu.make_async_copy(u_hbm, u_set.at[own_group], ld_sem.at[2])
     load_u.start()
-    load_s.start()
+    load_s[0].start()
+    load_s[1].start()
     load_c.start()
 
     barrier = pltpu.get_barrier_semaphore()
-
-    def plane_peer(d):
-        q = lax.rem(plane * 2 + core + d, 2 * planes)
-        p = lax.div(q, 2)
-        return low * 2 + lax.rem(q, 2), p * highs + high
-
-    def greet(d, carry):
-        pl.semaphore_signal(barrier, inc=1, device_id=plane_peer(d), device_id_type=MESH)
-        return carry
 
     across = (comp, other_feat)
     right = (comp + 2, feat)
@@ -118,6 +128,17 @@
     def signal(semaphore, device):
         pl.semaphore_signal(semaphore, inc=1, device_id=device, device_id_type=MESH)
 
+    @pl.when(count > 0)
+    def _():
+        def greet(k, carry):
+            @pl.when(k != itself)
+            def _():
+                signal(barrier, (comp, plane_at(k) * highs + high))
+
+            return carry
+
+        lax.fori_loop(0, planes, greet, 0)
+
     signal(barrier, along(lows // 2))
     signal(barrier, along(-(lows // 2)))
 
@@ -139,7 +160,7 @@
     def _():
         signal(barrier, left)
 
-    lax.fori_loop(1, 2 * planes, greet, 0)
+    signal(barrier, partner)
 
     u_pad[0:group, :] = jnp.zeros((group, width), jnp.float32)
     u_pad[2 * group : 3 * group, :] = jnp.zeros((group, width), jnp.float32)
@@ -150,18 +171,19 @@
         piece = u_own[:, b * 128 : (b + 1) * 128]
         squares = squares + piece * piece
     squares = jnp.concatenate([squares, squares], axis=0)
-    p_v[tiles - 1] = dot(jnp.ones((8, 128), jnp.float32), squares, 1, 1)
-    load_s.wait()
-    projected = dot(s_v[0:half, :], u_pad[group : 3 * group, :], 1, 1) + dot(
-        s_v[half:rows, :], u_pad[0 : 2 * group, :], 1, 1
-    )
+    p_v[tiles - 1] = dot_exact(jnp.ones((8, 128), jnp.float32), squares, 1, 1)
+    load_s[0].wait()
+    projected = dot(s_v[0:half, :], u_pad[group : 3 * group, :], 1, 1)
+    load_s[1].wait()
+    projected = projected + dot(s_v[half:rows, :], u_pad[0 : 2 * group, :], 1, 1)
     for t in range(tiles - 1):
         p_v[t] = projected[8 * t : 8 * t + 8, :]
 
     pl.semaphore_wait(
         barrier,
-        2 * planes
-        + jnp.where(even, 4, 2).astype(jnp.int32)
+        len(set(owners))
+        + jnp.where(count > 0, 0, 1).astype(jnp.int32)
+        + jnp.where(even, 5, 3).astype(jnp.int32)
         + jnp.where(heads, 1, 0).astype(jnp.int32),
     )
 
@@ -245,20 +267,21 @@
 
     place = core * tiles + first_tile
 
-    def spread_side(n, side_):
+    def add_planes(n, side_):
         for slot in range(n):
             total = zr_v[side_, 0, slot] + zr_v[side_, 1, slot]
-            tot_v[side_, slot] = total
-            x_v[side_, place + slot] = total
-
+            tot_v[slot, side_] = total
+            x_v[place + slot, side_] = total
+
+    def spread(n, source, target):
         def spread_start(k, carry):
             @pl.when(k != itself)
             def _():
                 pltpu.make_async_remote_copy(
-                    src_ref=tot_v.at[side_, pl.ds(0, n)],
-                    dst_ref=x_v.at[side_, pl.ds(place, n)],
-                    send_sem=ag_send.at[side_],
-                    recv_sem=ag_recv.at[side_],
+                    src_ref=source,
+                    dst_ref=target,
+                    send_sem=ag_send,
+                    recv_sem=ag_recv,
                     device_id=(comp, plane_at(k) * highs + high),
                     device_id_type=MESH,
                 ).start()
@@ -272,13 +295,18 @@
         @pl.when(count == n)
         def _():
             crossed(n, side, 1 - high)
-            spread_side(n, side)
+            add_planes(n, side)
 
             @pl.when(heads)
             def _():
                 crossed(n, 0, 0)
                 crossed(n, 0, 1)
-                spread_side(n, 0)
+                add_planes(n, 0)
+                spread(n, tot_v.at[pl.ds(0, n)], x_v.at[pl.ds(place, n)])
+
+            @pl.when(jnp.logical_not(heads))
+            def _():
+                spread(n, tot_v.at[pl.ds(0, n), side], x_v.at[pl.ds(place, n), side])
 
     borrowed(side, 1 - core)
 
@@ -286,50 +314,61 @@
     def _():
         borrowed(0, 1 - core)
 
-    def pass_on(side_):
-        tiles_here = pl.ds(core * tiles, tiles)
+    def pass_on(tiles_here):
         return pltpu.make_async_remote_copy(
-            src_ref=x_v.at[side_, tiles_here],
-            dst_ref=x_v.at[side_, tiles_here],
-            send_sem=xr_send.at[side_],
-            recv_sem=xr_recv.at[side_],
+            src_ref=tiles_here,
+            dst_ref=tiles_here,
+            send_sem=xr_send,
+            recv_sem=xr_recv,
             device_id=partner,
             device_id_type=MESH,
         )
 
-    def collect(side_):
+    my_tiles = pl.ds(core * tiles, tiles)
+    their_tiles = pl.ds((1 - core) * tiles, tiles)
+
+    @pl.when(heads)
+    def _():
         for n in range(slots + 1):
 
             @pl.when(count == n)
             def _():
-                landed(x_v.at[side_, pl.ds(0, tiles - n)], ag_recv.at[side_])
-
-        pass_on(side_).start()
-
-    collect(side)
-
-    @pl.when(heads)
-    def _():
-        collect(0)
-
-    def gather_side(side_):
-        landed(x_v.at[side_, pl.ds((1 - core) * tiles, tiles)], xr_recv.at[side_])
+                landed(x_v.at[pl.ds(0, tiles - n)], ag_recv)
+
+        pass_on(x_v.at[my_tiles]).start()
+        landed(x_v.at[their_tiles], xr_recv)
+
+    @pl.when(jnp.logical_not(heads))
+    def _():
+        for n in range(slots + 1):
+
+            @pl.when(count == n)
+            def _():
+                landed(x_v.at[pl.ds(0, tiles - n), side], ag_recv)
+
+        pass_on(x_v.at[my_tiles, side]).start()
+        landed(x_v.at[their_tiles, side], xr_recv)
 
     lane = lax.broadcasted_iota(jnp.int32, (8, 128), 1)
     eye = lax.broadcasted_iota(jnp.int32, (128, 128), 0) == lax.broadcasted_iota(jnp.int32, (128, 128), 1)
 
     def prepare(side_):
-        gather_side(side_)
-        scale0 = lax.rsqrt(x_v[side_, tiles - 1] / features + epsilon)
-        scale1 = lax.rsqrt(x_v[side_, 2 * tiles - 1] / features + epsilon)
+        scale0 = lax.rsqrt(x_v[tiles - 1, side_] / features + epsilon)
+        scale1 = lax.rsqrt(x_v[2 * tiles - 1, side_] / features + epsilon)
         scale_row = jnp.where(lane < group, scale0, scale1)
         for t in range(tiles - 1):
-            x0 = x_v[side_, t] * scale0 / root
-            x1 = x_v[side_, tiles + t] * scale1 / root
+            x0 = x_v[t, side_] * scale0 / root
+            x1 = x_v[tiles + t, side_] * scale1 / root
             a = jnp.where(lane < group, x0, pltpu.roll(x1, 64, 1))
             b = jnp.where(lane < group, pltpu.roll(x0, 64, 1), x1)
             xt_v[side_, pl.ds(8 * t, 8), :] = a
             xt_v[side_, pl.ds(half + 8 * t, 8), :] = b
+            xs_v[side_, pl.ds(8 * t, 8), :] = jnp.where(core == 0, a, b) * scale_row
+
+    def prepare_vectors(side_):
+        scale0 = lax.rsqrt(x_v[tiles - 1, side_] / features + epsilon)
+        scale1 = lax.rsqrt(x_v[2 * tiles - 1, side_] / features + epsilon)
+        scale_row = jnp.where(lane < group, scale0, scale1)
         scale_col = jnp.sum(
             jnp.where(eye, jnp.broadcast_to(scale_row[0:1, :], (128, 128)), 0.0), axis=1, keepdims=True
         )
@@ -345,12 +384,11 @@
 
     def add_own(b):
         columns = pl.ds(pl.multiple_of(b * 128, 128), 128)
-        here = pl.ds(my_rows, half)
-        own_v[b] = dot(xt_v[0, here, :], v_v[0, :, columns], 1, 0)
+        own_v[b] = dot(xs_v[0], u_set[0:128, columns], 1, 0)
 
         @pl.when(heads)
         def _():
-            own_v[b] = own_v[b] + dot(xt_v[1, here, :], v_v[1, :, columns], 1, 0)
+            own_v[b] = own_v[b] + dot(xs_v[1], u_set[128:256, columns], 1, 0)
 
     @pl.when(jnp.logical_and(forwards, fed))
     def _():
@@ -363,6 +401,14 @@
     my_group = pl.ds(pl.multiple_of(core * group, 8), group)
 
     def base():
+        @pl.when(odd)
+        def _():
+            prepare_vectors(1)
+
+        @pl.when(jnp.logical_or(even, heads))
+        def _():
+            prepare_vectors(0)
+
         x_own = xt_v[side]
         xtt_v[...] = x_own.T
         x_mine = xtt_v[my_group, :]
@@ -500,8 +546,8 @@
 
     lax.fori_loop(0, planes, tell_across, 0)
     lax.fori_loop(0, planes, tell_plane, 0)
-    store = pltpu.make_async_copy(new_v, out_hbm, ld_sem.at[0])
-    store.start()
+    for b in range(blocks):
+        pltpu.make_async_copy(new_v.at[:, pl.ds(b * 128, 128)], out_hbm.at[b], ld_sem.at[0]).start()
 
     for n in range(slots + 1):
 
@@ -519,11 +565,13 @@
     def _():
         lend(0, core, 1, partner).wait_send()
 
-    pass_on(side).wait_send()
-
     @pl.when(heads)
     def _():
-        pass_on(0).wait_send()
+        pass_on(x_v.at[my_tiles]).wait_send()
+
+    @pl.when(jnp.logical_not(heads))
+    def _():
+        pass_on(x_v.at[my_tiles, side]).wait_send()
 
     for n in range(1, slots + 1):
 
@@ -537,11 +585,11 @@
             def _():
                 landed(sent_v.at[pl.ds(0, n)], z_send)
 
-            landed(sent_v.at[pl.ds(0, n * (planes - 1))], ag_send.at[side])
+            landed(sent_v.at[pl.ds(0, n * (planes - 1))], ag_send)
 
             @pl.when(heads)
             def _():
-                landed(sent_v.at[pl.ds(0, n * (planes - 1))], ag_send.at[0])
+                landed(sent_v.at[pl.ds(0, n * (planes - 1))], ag_send)
 
     @pl.when(forwards)
     def _():
@@ -565,11 +613,11 @@
             / features
             + epsilon
         ),
-        (group, width),
+        (group, 128),
     )
 
     landed(fin_v.at[pl.ds(0, feats - 1)], fin_send)
-    store.wait()
+    landed(out_hbm, ld_sem.at[0])
 
 
 def step(planes, highs, lows, sub, owners, samples, start_vectors):
@@ -586,8 +634,8 @@
     updated, scale = pl.pallas_call(
         functools.partial(kernel, planes, highs, lows, sub, owners, width * feats),
         out_shape=(
-            jax.ShapeDtypeStruct((group, width), f32),
-            jax.ShapeDtypeStruct((group, width), f32),
+            jax.ShapeDtypeStruct((blocks, group, 128), f32),
+            jax.ShapeDtypeStruct((group, 128), f32),
         ),
         in_specs=[pl.BlockSpec(memory_space=pl.ANY)] * 2,
         out_specs=(pl.BlockSpec(memory_space=pl.ANY), pl.BlockSpec(memory_space=pltpu.VMEM)),
@@ -600,27 +648,28 @@
             pltpu.VMEM((slots, planes, 8, 128), f32),
             pltpu.VMEM((slots, 8, 128), f32),
             pltpu.VMEM((2, 2, slots, 8, 128), f32),
-            pltpu.VMEM((2, slots, 8, 128), f32),
-            pltpu.VMEM((2, 2 * tiles, 8, 128), f32),
+            pltpu.VMEM((slots, 2, 8, 128), f32),
+            pltpu.VMEM((2 * tiles, 2, 8, 128), f32),
             pltpu.VMEM((2, 2 * group, width), f32),
             pltpu.VMEM((2, rows, 128), f32),
+            pltpu.VMEM((2, half, 128), f32),
             pltpu.VMEM((128, rows), f32),
             pltpu.VMEM((blocks, half, 128), f32),
             pltpu.VMEM((blocks, rows, 128), f32),
             pltpu.VMEM((blocks, half, 128), f32),
             pltpu.VMEM((feats, 1, 128), f32),
             pltpu.VMEM((slots * planes, 8, 128), f32),
-            dma((3,)),
+            dma((4,)),
             dma((2,)),
             dma((2, 2)),
             dma,
             dma,
             dma,
             dma((2, 2)),
-            dma((2,)),
-            dma((2,)),
-            dma((2,)),
-            dma((2,)),
+            dma,
+            dma,
+            dma,
+            dma,
             dma,
             dma,
             dma((chunks,)),
@@ -630,9 +679,9 @@
             dma,
             pltpu.SemaphoreType.REGULAR,
         ],
-        compiler_params=pltpu.CompilerParams(collective_id=0, has_side_effects=True, vmem_limit_bytes=54700 * 1024),
+        compiler_params=pltpu.CompilerParams(collective_id=0, has_side_effects=True, vmem_limit_bytes=54900 * 1024),
     )(samples, start_vectors)
-    return updated * scale
+    return (updated * scale).transpose(1, 0, 2).reshape(group, width)
 
 
 def solution(mesh, sub=SUB, owners=OWNERS, planes=16, highs=2, lows=8):

time: 56.1 us -> 55.9 us (level)
    mul x1 -> x0, other arithmetic: 0.71 us -> none  [step(): return updated * scale]
    reshape x0 -> x1, other arithmetic: none -> 0.71 us  [step(): return (updated * scale).transpose(1, 0, 2).reshape(group, width)]
where the time goes in v4:
time: 55.9 us; the launch traced here: 55.7 us
  Pallas kernels  55 us (98%)
  other arithmetic  0.71 us (1%)
    pallas_call x1, Pallas kernels, step(): pl.pallas_call(functools.partial(kernel, planes, highs, lows, sub, owners...  55 us

profile of v4, /device:TPU:128, one launch (start us, length us, event | category | flops | bytes accessed | tf_op | source)
XLA Modules:
  0.0 55.7 jit_solution(1878487550824315776)
XLA Ops:
  0.0 55.0 %shard_map.28 = (f32[7,64,128]{2,1,0:T(8,128)S(1)}, f32[64,128]{1,0:T(8,128)S(1)}) custom-call(f32[1,192,896]{2,1,0:T(8,128)} %s_hbm.1, f32[64,896]{1,0:T(8,128)} %u_hbm.1), custom_call_target="tpu_custom_call" | custom-call | tf_op jit(solution)/shard_map/pallas_call | solution.py:634
  55.0 0.7 %copy_bitcast_fusion = f32[64,896]{1,0:T(8,128)} fusion(f32[7,64,128]{2,1,0:T(8,128)S(1)} %get-tuple-element.7, f32[64,128]{1,0:T(8,128)S(1)} %get-tuple-element.8), kind=kLoop, calls=%fused_computation | loop fusion | flops 57344 | bytes 491520 | tf_op jit(solution)/shard_map/reshape | solution.py:684

commit v5 on v4

--- a/solution.py
+++ b/solution.py
@@ -14,7 +14,7 @@
 highest = lax.Precision.HIGHEST
 
 SUB = 24
-OWNERS = (10, 10, 6, 6, 9, 11, 14, 2, 5, 7, 8, 13, 15)
+OWNERS = (10, 10, 10, 6, 6, 6, 9, 9, 9, 11, 11, 14, 14)
 
 
 def dot_exact(a, b, ca, cb):

time: 55.9 us -> 55.6 us (level)
  no operation moved by 1% of the time
where the time goes in v5:
time: 55.6 us; the launch traced here: 55.5 us
  Pallas kernels  54.8 us (99%)
  other arithmetic  0.71 us (1%)
    pallas_call x1, Pallas kernels, step(): pl.pallas_call(functools.partial(kernel, planes, highs, lows, sub, owners...  54.8 us

profile of v5, /device:TPU:128, one launch (start us, length us, event | category | flops | bytes accessed | tf_op | source)
XLA Modules:
  0.0 55.5 jit_solution(10304420144439659601)
XLA Ops:
  0.0 54.8 %shard_map.28 = (f32[7,64,128]{2,1,0:T(8,128)S(1)}, f32[64,128]{1,0:T(8,128)S(1)}) custom-call(f32[1,192,896]{2,1,0:T(8,128)} %s_hbm.1, f32[64,896]{1,0:T(8,128)} %u_hbm.1), custom_call_target="tpu_custom_call" | custom-call | tf_op jit(solution)/shard_map/pallas_call | solution.py:634
  54.8 0.7 %copy_bitcast_fusion = f32[64,896]{1,0:T(8,128)} fusion(f32[7,64,128]{2,1,0:T(8,128)S(1)} %get-tuple-element.7, f32[64,128]{1,0:T(8,128)S(1)} %get-tuple-element.8), kind=kLoop, calls=%fused_computation | loop fusion | flops 57344 | bytes 491520 | tf_op jit(solution)/shard_map/reshape | solution.py:684

commit v6 on v5

--- a/solution.py
+++ b/solution.py
@@ -237,7 +237,10 @@
     def crossed(n, side_, high_):
         landed(zr_v.at[side_, high_, pl.ds(0, n)], z_recv.at[side_, high_])
 
-    pl.semaphore_wait(ready, 2)
+    @pl.when(count == 0)
+    def _():
+        pl.semaphore_wait(ready, 2)
+
     for n in range(1, slots + 1):
 
         @pl.when(count == n)
@@ -250,6 +253,7 @@
                 for p in range(1, planes):
                     total = total + rs_v[slot, p]
                 zs_v[slot] = total
+            pl.semaphore_wait(ready, 2)
             exchange(n, across).start()
 
             @pl.when(lends)

time: 55.6 us -> 55.6 us (level)
  no operation moved by 1% of the time
where the time goes in v6:
time: 55.6 us; the launch traced here: 55.5 us
  Pallas kernels  54.8 us (99%)
  other arithmetic  0.71 us (1%)
    pallas_call x1, Pallas kernels, step(): pl.pallas_call(functools.partial(kernel, planes, highs, lows, sub, owners...  54.8 us

profile of v6, /device:TPU:128, one launch (start us, length us, event | category | flops | bytes accessed | tf_op | source)
XLA Modules:
  0.0 55.5 jit_solution(10518607689805085710)
XLA Ops:
  0.0 54.8 %shard_map.28 = (f32[7,64,128]{2,1,0:T(8,128)S(1)}, f32[64,128]{1,0:T(8,128)S(1)}) custom-call(f32[1,192,896]{2,1,0:T(8,128)} %s_hbm.1, f32[64,896]{1,0:T(8,128)} %u_hbm.1), custom_call_target="tpu_custom_call" | custom-call | tf_op jit(solution)/shard_map/pallas_call | solution.py:638
  54.8 0.7 %copy_bitcast_fusion = f32[64,896]{1,0:T(8,128)} fusion(f32[7,64,128]{2,1,0:T(8,128)S(1)} %get-tuple-element.7, f32[64,128]{1,0:T(8,128)S(1)} %get-tuple-element.8), kind=kLoop, calls=%fused_computation | loop fusion | flops 57344 | bytes 491520 | tf_op jit(solution)/shard_map/reshape | solution.py:688

commit v7 on v6

--- a/solution.py
+++ b/solution.py
@@ -128,6 +128,9 @@
     def signal(semaphore, device):
         pl.semaphore_signal(semaphore, inc=1, device_id=device, device_id_type=MESH)
 
+    signal(barrier, along(lows // 2))
+    signal(barrier, along(-(lows // 2)))
+
     @pl.when(count > 0)
     def _():
         def greet(k, carry):
@@ -138,9 +141,6 @@
             return carry
 
         lax.fori_loop(0, planes, greet, 0)
-
-    signal(barrier, along(lows // 2))
-    signal(barrier, along(-(lows // 2)))
 
     @pl.when(even)
     def _():

time: 55.6 us -> 55.6 us (level)
  no operation moved by 1% of the time
where the time goes in v7:
time: 55.6 us; the launch traced here: 55.5 us
  Pallas kernels  54.8 us (99%)
  other arithmetic  0.71 us (1%)
    pallas_call x1, Pallas kernels, step(): pl.pallas_call(functools.partial(kernel, planes, highs, lows, sub, owners...  54.8 us

profile of v7, /device:TPU:128, one launch (start us, length us, event | category | flops | bytes accessed | tf_op | source)
XLA Modules:
  0.0 55.5 jit_solution(3274397565526209011)
XLA Ops:
  0.0 54.8 %shard_map.28 = (f32[7,64,128]{2,1,0:T(8,128)S(1)}, f32[64,128]{1,0:T(8,128)S(1)}) custom-call(f32[1,192,896]{2,1,0:T(8,128)} %s_hbm.1, f32[64,896]{1,0:T(8,128)} %u_hbm.1), custom_call_target="tpu_custom_call" | custom-call | tf_op jit(solution)/shard_map/pallas_call | solution.py:638
  54.8 0.7 %copy_bitcast_fusion = f32[64,896]{1,0:T(8,128)} fusion(f32[7,64,128]{2,1,0:T(8,128)S(1)} %get-tuple-element.7, f32[64,128]{1,0:T(8,128)S(1)} %get-tuple-element.8), kind=kLoop, calls=%fused_computation | loop fusion | flops 57344 | bytes 491520 | tf_op jit(solution)/shard_map/reshape | solution.py:688
